TPU v7x, 256 devices: a whole 4x4x8 slice. The times are simulated.
256 devices in a mesh: op: 8 (over z_lo, core), sec: 32 (over y, x, z_hi).
Axes of the slice: x: 4, y: 4, z: 8 (z_hi: 2, z_lo: 4; z = z_hi * 4 + z_lo), core: 2. Of those that a mesh axis runs over, the one named last changes fastest.
Arguments:
- psi: bfloat16 [3, 256, 256, 256], P(None, 'sec'), may hold values from -6 to 6
- left_ops: bfloat16 [32, 256, 256, 256], P('op', 'sec'), may hold values from -0.0625 to 0.0625
- right_ops: bfloat16 [32, 256, 256, 256], P('op', 'sec'), may hold values from -0.375 to 0.375
- shifts: int32 [32], P('op'), may hold values from -1 to 1
- active: int32 [32, 256], P('op', 'sec'), may hold values 0 or 1
Outputs:
- right_view: bfloat16 [3, 256, 256, 256], P(None, 'sec', None, 'op')
All inputs are finite; a program needn't handle non-finite values. No bound on the sum of `active` on one device may be relied on, other than what follows from the above.
Results may differ from a plain program's by a relative error of at most 0.0049.
Values may be sent and summed in bfloat16 or wider, within the bound.
A program may use at most 64 MiB of HBM per device.

v0:
```python
import jax
import jax.numpy as jnp
from jax import lax
from jax.sharding import PartitionSpec as P

QMAX = 1


def extended(value, sides, width):
    for axis, dim in sides:
        size, length = (lax.axis_size(axis), value.shape[dim])
        up = [(i, (i + 1) % size) for i in range(size - 1)]
        down = [(j, i) for i, j in up]
        last = lax.slice_in_dim(value, length - width, length, axis=dim)
        leading = lax.slice_in_dim(value, 0, width, axis=dim)
        before = lax.ppermute(last, axis, up)
        after = lax.ppermute(leading, axis, down)
        value = jnp.concatenate([before, value, after], axis=dim)
    return value


def per_device(psi, left_ops, right_ops, shifts, active):
    padded = extended(psi, (("sec", 1),), QMAX)
    count = left_ops.shape[0]
    sectors = psi.shape[1]
    nvec = psi.shape[0]
    blk = psi.shape[2]

    def add_term(index, total):
        start = QMAX - shifts[index]
        source = lax.dynamic_slice_in_dim(padded, start, sectors, 1)
        middle = jnp.einsum(
            "tij,vtjk->vtik", left_ops[index], source, preferred_element_type=jnp.float32
        ).astype(jnp.bfloat16)
        term = jnp.einsum(
            "vtik,tlk->vlti", middle, right_ops[index], preferred_element_type=jnp.float32
        )
        weight = active[index].astype(jnp.float32)
        return total + term * weight[None, None, :, None]

    total = lax.fori_loop(0, count, add_term, jnp.zeros((nvec, blk, sectors, blk), jnp.float32))
    summed = lax.psum(total, "op")
    share = blk // lax.axis_size("op")
    owned = lax.dynamic_slice_in_dim(summed, lax.axis_index("op") * share, share, 3)
    return lax.all_to_all(
        owned.astype(jnp.bfloat16), "sec", split_axis=1, concat_axis=2, tiled=True
    )


def solution(mesh):
    placed = (
        P(None, "sec", None, None),
        P("op", "sec", None, None),
        P("op", "sec", None, None),
        P("op"),
        P("op", "sec"),
    )
    return jax.shard_map(
        per_device,
        mesh=mesh,
        in_specs=placed,
        out_specs=P(None, "sec", None, "op"),
        check_vma=False,
    )
```

profile of v0, /device:TPU:1, one launch (start us, length us, event | category | flops | bytes accessed | tf_op | source)
XLA Modules:
  0.0 268.5 jit_solution(1910352454193892259)
XLA Ops:
  0.0 3.2 %copy.17 = bf16[3,8,256,256]{2,3,0,1:T(8,128)(2,1)S(1)} copy(bf16[3,8,256,256]{3,2,1,0:T(8,128)(2,1)} %param.7) | data formatting | bytes 6291456 | tf_op args[0]
  3.2 0.8 fusion.23
  4.0 10.4 %collective-permute-start = (bf16[3,1,256,256]{2,3,0,1:T(8,128)(2,1)}, bf16[3,1,256,256]{2,3,0,1:T(8,128)(2,1)}, u32[]{:S(2)}, u32[]{:S(2)}) collective-permute-start(bf16[3,1,256,256]{2,3,0,1:T(8,128)(2,1)} %get-tuple-element.220), channel_id=1, source_target_pairs={{0,1},{1,2},{2,3},{3,4},{4,5},{5,6},{6,7},{7,8},{8,9},{9,10},{10,1... | collective-permute-start | bytes 1179656 | tf_op jit(solution)/shard_map/ppermute | solution.py:16
  14.4 1.3 collective-permute-start.1
  15.7 0.0 copy-start
  15.7 7.2 %collective-permute-done = bf16[3,1,256,256]{2,3,0,1:T(8,128)(2,1)} collective-permute-done((bf16[3,1,256,256]{2,3,0,1:T(8,128)(2,1)}, bf16[3,1,256,256]{2,3,0,1:T(8,128)(2,1)}, u32[]{:S(2)}, u32[]{:S(2)}) %collective-permute-start) | collective-permute-done | bytes 393248 | tf_op jit(solution)/shard_map/ppermute | solution.py:16
  22.9 16.8 %collective-permute-done.1 = bf16[3,1,256,256]{2,3,0,1:T(8,128)(2,1)} collective-permute-done((bf16[3,1,256,256]{2,3,0,1:T(8,128)(2,1)S(1)}, bf16[3,1,256,256]{2,3,0,1:T(8,128)(2,1)}, u32[]{:S(2)}, u32[]{:S(2)}) %collective-permute-start.1) | collective-permute-done | bytes 393248 | tf_op jit(solution)/shard_map/ppermute | solution.py:17
  39.7 3.2 %pad_maximum_fusion = bf16[3,10,256,256]{2,3,0,1:T(8,128)(2,1)} fusion(bf16[3,1,256,256]{2,3,0,1:T(8,128)(2,1)} %collective-permute-done.1, bf16[3,8,256,256]{2,3,0,1:T(8,128)(2,1)S(1)} %copy.17, bf16[3,1,256,256]{2,3,0,1:T(8,128)(2,1)} %collective-permute-done), kind=kLoop, calls=%fused_computation.14 | loop fusion | flops 3932160 | bytes 7864320 | tf_op jit(solution)/shard_map/concatenate | solution.py:18
  42.9 0.0 copy-done
  42.9 44.0 %while.16 = (s32[]{:T(128)}, f32[3,256,8,256]{3,1,0,2:T(8,128)}, bf16[4,8,256,256]{3,2,1,0:T(8,128)(2,1)}, s32[4]{0:T(128)S(1)}, bf16[3,10,256,256]{2,3,0,1:T(8,...) while((s32[]{:T(128)}, f32[3,256,8,256]{3,1,0,2:T(8,128)}, ...), condition=%wide.region_1.0_spmd.clone, body=%wide.region_0.0_spmd.clone.sunk | while | flops 1616904192 | bytes 17827096 | solution.py:41
  42.9 0.6 dynamic_slice.93
  44.8 0.7 fusion.34
  45.5 7.0 %bitcast_add_fusion.2 = f32[3,256,8,256]{3,1,0,2:T(8,128)} fusion(f32[3,256,8,256]{3,1,0,2:T(8,128)} %get-tuple-element.277, f32[8]{0:T(128)S(1)} %fusion.34, pred[]{:T(512)S(6)} %compare.3, bf16[3,10,256,256]{2,3,0,1:T(8,128)(2,1)} %get-tuple-element.291, s32[]{:T(128)S(6)} %select_n.27, bf16[4,8,256,256]{3,2,1,0:T(8,128)(2,1)} %get-tuple-element.292, ...), kind=kOutput, calls=%fused_computation.clone.1 | convolution fusion | flops 1616904192 | bytes 17826852 | tf_op jit(solution)/shard_map/while/body/eval_jaxpr/vtik,tlk->vlti/dot_general | solution.py:35
  52.5 0.6 dynamic_slice.93
  54.4 0.7 fusion.34
  55.1 8.9 %bitcast_add_fusion.2 = f32[3,256,8,256]{3,1,0,2:T(8,128)} fusion(f32[3,256,8,256]{3,1,0,2:T(8,128)} %get-tuple-element.277, f32[8]{0:T(128)S(1)} %fusion.34, pred[]{:T(512)S(6)} %compare.3, bf16[3,10,256,256]{2,3,0,1:T(8,128)(2,1)} %get-tuple-element.291, s32[]{:T(128)S(6)} %select_n.27, bf16[4,8,256,256]{3,2,1,0:T(8,128)(2,1)} %get-tuple-element.292, ...), kind=kOutput, calls=%fused_computation.clone.1 | convolution fusion | flops 1616904192 | bytes 17826852 | tf_op jit(solution)/shard_map/while/body/eval_jaxpr/vtik,tlk->vlti/dot_general | solution.py:35
  64.0 0.6 dynamic_slice.93
  65.9 0.7 fusion.34
  66.6 8.9 %bitcast_add_fusion.2 = f32[3,256,8,256]{3,1,0,2:T(8,128)} fusion(f32[3,256,8,256]{3,1,0,2:T(8,128)} %get-tuple-element.277, f32[8]{0:T(128)S(1)} %fusion.34, pred[]{:T(512)S(6)} %compare.3, bf16[3,10,256,256]{2,3,0,1:T(8,128)(2,1)} %get-tuple-element.291, s32[]{:T(128)S(6)} %select_n.27, bf16[4,8,256,256]{3,2,1,0:T(8,128)(2,1)} %get-tuple-element.292, ...), kind=kOutput, calls=%fused_computation.clone.1 | convolution fusion | flops 1616904192 | bytes 17826852 | tf_op jit(solution)/shard_map/while/body/eval_jaxpr/vtik,tlk->vlti/dot_general | solution.py:35
  75.5 0.6 dynamic_slice.93
  77.3 0.7 fusion.34
  78.0 8.9 %bitcast_add_fusion.2 = f32[3,256,8,256]{3,1,0,2:T(8,128)} fusion(f32[3,256,8,256]{3,1,0,2:T(8,128)} %get-tuple-element.277, f32[8]{0:T(128)S(1)} %fusion.34, pred[]{:T(512)S(6)} %compare.3, bf16[3,10,256,256]{2,3,0,1:T(8,128)(2,1)} %get-tuple-element.291, s32[]{:T(128)S(6)} %select_n.27, bf16[4,8,256,256]{3,2,1,0:T(8,128)(2,1)} %get-tuple-element.292, ...), kind=kOutput, calls=%fused_computation.clone.1 | convolution fusion | flops 1616904192 | bytes 17826852 | tf_op jit(solution)/shard_map/while/body/eval_jaxpr/vtik,tlk->vlti/dot_general | solution.py:35
  86.9 9.1 %copy.20 = f32[3,256,8,256]{3,2,0,1:T(8,128)} copy(f32[3,256,8,256]{3,1,0,2:T(8,128)} %get-tuple-element.181) | data formatting | bytes 12582912 | tf_op jit(solution)/shard_map/while | solution.py:41
  96.0 132.5 %all-reduce.1 = bf16[3,256,8,256]{3,2,0,1:T(8,128)(2,1)S(1)} all-reduce(f32[3,256,8,256]{3,2,0,1:T(8,128)} %copy.20), channel_id=1, replica_groups=mesh['op'=8,'sec'=32] {'op'}, use_global_device_ids=true, to_apply=%region_2.0 | all-reduce | flops 1572864 | bytes 9437184 | tf_op jit(solution)/shard_map/psum | solution.py:42
  228.5 1.7 fusion.24
  230.2 3.1 %reshape.17 = bf16[32,2,3072]{2,1,0:T(2,128)(2,1)S(1)} reshape(bf16[256,3,8,32]{3,2,1,0:T(8,128)(2,1)} %fusion.24) | data formatting | bytes 786432
  233.2 32.8 %all_to_all.18 = bf16[32,2,3072]{2,1,0:T(2,128)(2,1)S(1)} all-to-all(bf16[32,2,3072]{2,1,0:T(2,128)(2,1)S(1)} %reshape.17), channel_id=1, replica_groups=mesh['op'=8,'sec'=32] {'sec'}, dimensions={0} | all-to-all | bytes 786432 | tf_op jit(solution)/shard_map/all_to_all | solution.py:45
  266.0 0.7 reshape.18
  266.8 0.4 copy.27
  267.2 1.3 copy.22
  (1 shorter events, 0.0 us)
Async XLA Ops:
  4.0 18.9 %collective-permute-start = (bf16[3,1,256,256]{2,3,0,1:T(8,128)(2,1)}, bf16[3,1,256,256]{2,3,0,1:T(8,128)(2,1)}, u32[]{:S(2)}, u32[]{:S(2)}) collective-permute-start(bf16[3,1,256,256]{2,3,0,1:T(8,128)(2,1)} %get-tuple-element.220), channel_id=1, source_target_pairs={{0,1},{1,2},{2,3},{3,4},{4,5},{5,6},{6,7},{7,8},{8,9},{9,10},{10,1... | collective-permute-start | bytes 1179656 | tf_op jit(solution)/shard_map/ppermute | solution.py:16
  14.4 25.3 %collective-permute-start.1 = (bf16[3,1,256,256]{2,3,0,1:T(8,128)(2,1)S(1)}, bf16[3,1,256,256]{2,3,0,1:T(8,128)(2,1)}, u32[]{:S(2)}, u32[]{:S(2)}) collective-permute-start(bf16[3,1,256,256]{2,3,0,1:T(8,128)(2,1)S(1)} %get-tuple-element.221), channel_id=1, source_target_pairs={{1,0},{2,1},{3,2},{4,3},{5,4},{6,5},{7,6},{8,7},{9,8},{10,9},{11,1... | collective-permute-start | bytes 1179656 | tf_op jit(solution)/shard_map/ppermute | solution.py:17
  15.7 27.2 %copy-start = (s32[4]{0:T(128)S(1)}, s32[4]{0:T(128)}, u32[]{:S(2)}) copy-start(s32[4]{0:T(128)} %param.10) | copy-start | bytes 52
where the time goes:
time: 269 us
  blocking collectives  165 us (61%)
  matrix products  33.7 us (13%)
  waiting for transfers between devices  24 us (9%)
  local copies, waits for them, and re-layouts  22.6 us (8%)
  starting transfers between devices  11.7 us (4%)
  other arithmetic  6 us (2%)
  loops' own time  5.21 us (2%)
    psum x1, blocking collectives, per_device(): summed = lax.psum(total, 'op')  132 us
    dot_general x4, matrix products, add_term(): jnp.einsum('vtik,tlk->vlti', middle, right_ops[index], preferred_element_...  33.7 us
    all_to_all x1, blocking collectives, per_device(): lax.all_to_all(owned.astype(jnp.bfloat16), 'sec', split_axis=1, concat_ax...  32.8 us
    ppermute x1, waiting for transfers between devices, extended(): after = lax.ppermute(leading, axis, down)  16.8 us
    ppermute x1, starting transfers between devices, extended(): before = lax.ppermute(last, axis, up)  10.4 us
    while x1, local copies, waits for them, and re-layouts, per_device(): lax.fori_loop(0, count, add_term, jnp.zeros((nvec, blk, sectors, blk), jn...  9.08 us
    unnamed x6, local copies, waits for them, and re-layouts  8.67 us
    ppermute x1, waiting for transfers between devices, extended(): before = lax.ppermute(last, axis, up)  7.21 us
  transfers between devices with their start and end apart: 2, of which 2 were waited for; matrix products, arithmetic and copies ran while one was open for 0% of the time, Pallas kernels for 0%

commit v1 on v0

v1 whole, which is shorter than its diff:
```python
import functools

import jax
import jax.numpy as jnp
from jax import lax
from jax.experimental import pallas as pl
from jax.experimental.pallas import tpu as pltpu
from jax.sharding import PartitionSpec as P

MESH = pl.DeviceIdType.MESH
F32 = jnp.float32
BF16 = jnp.bfloat16
LAG = 2


def kernel(
    nsec_total, sizes, shifts, active, psi_hbm, left_hbm, right_hbm, out_ref,
    psi, edge, left, right, perm, mid, rcat, acc,
    s0, r0, s1, keep, r1, s2, own, r2, turn, wide, wsend, wrecv,
    load_sem, op_sem, edge_sem, halo_send, halo_recv, sib_send, sib_recv,
    send0, recv0, send1, recv1, send2, recv2, send3, recv3, self_sem,
):
    nyx, count, nvec, sectors, blk = sizes
    op, sec = lax.axis_index("op"), lax.axis_index("sec")
    zl, core = lax.div(op, 2), lax.rem(op, 2)
    yx, zh = lax.div(sec, 2), lax.rem(sec, 2)
    z = zh * 4 + zl
    e = lax.rem(zl, 2)
    other = 1 - core
    nsec = 2 * nyx
    half = blk // 2

    def at(zz, yxx):
        zz = lax.rem(zz + 16, 8)
        return {"op": lax.rem(zz, 4) * 2 + core, "sec": yxx * 2 + lax.div(zz, 4)}

    sibling = {"op": zl * 2 + other, "sec": sec}
    partner = at(z + 1 - 2 * e, yx)
    sec_up, sec_down = lax.rem(sec + 1, nsec), lax.rem(sec + nsec - 1, nsec)
    ahead = {
        "op": jnp.where(zl == 3, core, op + 2),
        "sec": jnp.where(zl == 3, sec_up, sec),
    }
    behind = {
        "op": jnp.where(zl == 0, 6 + core, op - 2),
        "sec": jnp.where(zl == 0, sec_down, sec),
    }

    barrier = pltpu.get_barrier_semaphore()
    pl.semaphore_signal(barrier, inc=1, device_id=sibling, device_id_type=MESH)
    pl.semaphore_signal(barrier, inc=1, device_id=ahead, device_id_type=MESH)
    pl.semaphore_signal(barrier, inc=1, device_id=behind, device_id_type=MESH)

    @pl.loop(1, 8)
    def _(d):
        pl.semaphore_signal(barrier, inc=1, device_id=at(z + d, yx), device_id_type=MESH)

    @pl.loop(1, nyx)
    def _(d):
        pl.semaphore_signal(
            barrier, inc=1, device_id=at(z, lax.rem(yx + d, nyx)), device_id_type=MESH
        )

    load_psi = pltpu.make_async_copy(psi_hbm, psi, load_sem)
    load_psi.start()

    def sector_of(n):
        return jnp.where(n < sectors - 2, n + 1, jnp.where(n == sectors - 2, 0, sectors - 1))

    def load_ops(t):
        return (
            pltpu.make_async_copy(left_hbm.at[:, t], left.at[t], op_sem.at[0, t]),
            pltpu.make_async_copy(right_hbm.at[:, t], right.at[t], op_sem.at[1, t]),
        )

    @pl.loop(0, sectors)
    def _(n):
        for copy in load_ops(sector_of(n)):
            copy.start()

    edge_loads = (
        pltpu.make_async_copy(psi_hbm.at[:, 0:2], edge.at[0, :, 1:3], edge_sem.at[0]),
        pltpu.make_async_copy(
            psi_hbm.at[:, sectors - 2 : sectors], edge.at[1, :, 0:2], edge_sem.at[1]
        ),
    )
    for copy in edge_loads:
        copy.start()

    rows_each = blk // nsec
    row = lax.broadcasted_iota(jnp.int32, (blk, blk), 0)
    col = lax.broadcasted_iota(jnp.int32, (blk, blk), 1)
    inner = lax.rem(row, half)
    want = (
        lax.div(inner, rows_each) * (2 * rows_each)
        + lax.div(row, half) * rows_each
        + lax.rem(inner, rows_each)
    )
    perm[...] = jnp.where(col == want, 1.0, 0.0).astype(BF16)

    load_psi.wait()
    pl.semaphore_wait(barrier, 3 + 7 + nyx - 1)

    mine = pl.ds(core * half, half)

    def halo(side, v, source):
        return pltpu.make_async_remote_copy(
            src_ref=source,
            dst_ref=edge.at[side, v, 2 * side, mine],
            send_sem=halo_send.at[side, v],
            recv_sem=halo_recv.at[side, v],
            device_id=behind if side else ahead,
            device_id_type=MESH,
        )

    def share(side, v):
        return pltpu.make_async_remote_copy(
            src_ref=edge.at[side, v, 2 * side, mine],
            dst_ref=edge.at[side, v, 2 * side, mine],
            send_sem=sib_send.at[side, v],
            recv_sem=sib_recv.at[side, v],
            device_id=sibling,
            device_id_type=MESH,
        )

    @pl.when(zl == 3)
    def _():
        for v in range(nvec):
            halo(0, v, psi.at[v, sectors - 1, mine]).start()

    @pl.when(zl == 0)
    def _():
        for v in range(nvec):
            halo(1, v, psi.at[v, 0, mine]).start()

    def relay(side, n):
        place = (3 - zl) if side else zl
        v = n - place

        @pl.when((v >= 0) & (v < nvec))
        def _():
            here = edge.at[side, v, 2 * side, mine]
            halo(side, v, here).wait_recv()

            @pl.when(place < 3)
            def _():
                halo(side, v, here).start()

            share(side, v).start()

    def compute(t, slot, source):
        for k in range(count):
            shift = shifts[k]
            anchor = sec * sectors + t - shift
            good = (anchor >= 0) & (anchor < nsec_total)
            weight = jnp.where(good, active[k, t], 0).astype(F32)
            moved = jnp.dot(perm[...], right[t, k], preferred_element_type=F32)
            rcat[:, k * blk : (k + 1) * blk] = (moved * weight).astype(BF16)
            for v in range(nvec):
                mid[v, :, k * blk : (k + 1) * blk] = jnp.dot(
                    left[t, k], source(v, shift), preferred_element_type=F32
                ).astype(BF16)
        for v in range(nvec):
            acc[slot, v] = lax.dot_general(
                mid[v], rcat[...], (((1,), (1,)), ((), ())), preferred_element_type=F32
            ).reshape(4, 2, blk // 8, blk)

    def level0(t):
        return pltpu.make_async_remote_copy(
            src_ref=s0.at[t], dst_ref=r0.at[t], send_sem=send0.at[t], recv_sem=recv0.at[t],
            device_id=sibling, device_id_type=MESH,
        )

    def level1(t):
        return pltpu.make_async_remote_copy(
            src_ref=s1.at[t, e], dst_ref=r1.at[t], send_sem=send1.at[t], recv_sem=recv1.at[t],
            device_id=partner, device_id_type=MESH,
        )

    def level2(t, p):
        return pltpu.make_async_remote_copy(
            src_ref=s2.at[t, p - 1], dst_ref=r2.at[p - 1, t],
            send_sem=send2.at[t, p - 1], recv_sem=recv2.at[t, p - 1],
            device_id=at(z + jnp.where(e == 1, p, -p), yx), device_id_type=MESH,
        )

    def stage0(t, slot):
        s0[t] = acc[slot, :, :, other].astype(BF16)
        level0(t).start()

    def stage1(t, slot):
        level0(t).wait_recv()
        for zl2 in range(4):
            for zh2 in range(2):
                lanes = slice(zh2 * half, (zh2 + 1) * half)
                value = acc[slot, :, zl2, core, :, lanes] + r0[t, :, zl2, :, lanes].astype(F32)
                delta = lax.rem(zh2 * 4 + zl2 - (z - e) + 16, 8)
                low = (delta >= 1) & (delta <= 4)
                side = jnp.where(low, 0, 1)
                place = jnp.where(low, delta - 1, lax.rem(8 - delta, 8))
                s1[t, side, place] = value.astype(BF16)
                keep[t, side, place] = value
        level1(t).start()

    def stage2(t):
        level1(t).wait_recv()
        for p in range(4):
            value = keep[t, 1 - e, p] + r1[t, p].astype(F32)
            if p == 0:
                own[t] = value
            else:
                s2[t, p - 1] = value.astype(BF16)
                level2(t, p).start()

    @pl.loop(0, sectors + LAG)
    def _(n):
        slot = lax.rem(n, 2)

        @pl.when(n < sectors)
        def _():
            t = sector_of(n)
            for copy in load_ops(t):
                copy.wait()

            @pl.when(n < sectors - 2)
            def _():
                compute(t, slot, lambda v, shift: psi[v, t - shift])

            @pl.when(n == sectors - 2)
            def _():
                for copy in edge_loads:
                    copy.wait()
                for side in range(2):
                    for v in range(nvec):
                        share(side, v).wait_recv()

            @pl.when(n >= sectors - 2)
            def _():
                which = n - (sectors - 2)
                compute(t, slot, lambda v, shift: edge[which, v, 1 - shift])

            stage0(t, slot)

        @pl.when(n < sectors - 2)
        def _():
            relay(0, n)
            relay(1, n)

        @pl.when((n >= 1) & (n <= sectors))
        def _():
            stage1(sector_of(n - 1), 1 - slot)

        @pl.when(n >= LAG)
        def _():
            stage2(sector_of(n - LAG))

    near = jnp.where(lax.rem(e + lax.div(zl, 2), 2) == 1, 0, 1)
    for p in range(1, 4):
        @pl.loop(0, sectors)
        def _(t):
            level2(t, p).wait_recv()

    part = blk // 8
    for mine_group in (True, False):
        group = zh if mine_group else 1 - zh

        @pl.loop(0, nvec)
        def _(v):
            for quad in range(2):
                ts = slice(quad * 4, quad * 4 + 4)
                if mine_group:
                    value = own[ts, v] + r2[near, ts, v].astype(F32)
                else:
                    value = r2[1 - near, ts, v].astype(F32) + r2[2, ts, v].astype(F32)
                turn[quad] = value.reshape(4 * part, half).T
                for lq in range(2):
                    pieces = [turn[quad, pl.ds(lq * 4 + r, nyx, stride=8), :] for r in range(4)]
                    for t4 in range(4):
                        lanes = slice(t4 * part, (t4 + 1) * part)
                        joined = jnp.concatenate([piece[:, lanes] for piece in pieces], axis=1)
                        wide[group, v * 2 + lq, pl.ds(quad * 4 + t4, nyx, stride=8), :] = joined

    @pl.loop(0, nyx)
    def _(d):
        rows = pl.ds(pl.multiple_of(d * 8, 8), 8)
        for tile in range(6):
            both = [wide[group, tile, rows, :] for group in range(2)]
            lanes = slice(tile * 128, (tile + 1) * 128)
            wsend[d, :, lanes] = jnp.concatenate(both, axis=0).astype(BF16)

    def spread(d):
        far = lax.rem(yx + d, nyx)
        return pltpu.make_async_remote_copy(
            src_ref=wsend.at[far], dst_ref=wrecv.at[yx],
            send_sem=send3.at[d], recv_sem=recv3.at[d],
            device_id=at(z, far), device_id_type=MESH,
        )

    @pl.loop(1, nyx)
    def _(d):
        spread(d).start()

    keep_own = pltpu.make_async_copy(wsend.at[yx], wrecv.at[yx], self_sem)
    keep_own.start()
    keep_own.wait()

    @pl.loop(1, nyx)
    def _(d):
        spread(d).wait_recv()

    for h in range(2):
        for tile in range(6):
            lanes = slice(tile * 128, (tile + 1) * 128)
            value = wrecv[h * 8 : (h + 1) * 8, :, lanes].astype(F32).reshape(128, 128)
            out_ref[lanes, h * 128 : (h + 1) * 128] = value.T.astype(BF16)

    for side in range(2):
        for v in range(nvec):
            halo(side, v, psi.at[v, 0, mine]).wait_send()
            share(side, v).wait_send()

    @pl.loop(0, sectors)
    def _(t):
        level0(t).wait_send()
        level1(t).wait_send()
        for p in range(1, 4):
            level2(t, p).wait_send()

    @pl.loop(1, nyx)
    def _(d):
        spread(d).wait_send()


def solution(mesh):
    nsec = mesh.shape["sec"]
    nyx = nsec // 2

    def per_device(psi, left_ops, right_ops, shifts, active):
        nvec, sectors, blk = psi.shape[:3]
        count = left_ops.shape[0]
        part, half = blk // 8, blk // 2
        sizes = (nyx, count, nvec, sectors, blk)
        smem = pl.BlockSpec(memory_space=pltpu.SMEM)
        hbm = pl.BlockSpec(memory_space=pl.ANY)
        dma = pltpu.SemaphoreType.DMA
        result = pl.pallas_call(
            functools.partial(kernel, nsec * sectors, sizes),
            out_shape=jax.ShapeDtypeStruct((nvec * blk, blk), BF16),
            in_specs=[smem, smem, hbm, hbm, hbm],
            out_specs=pl.BlockSpec(memory_space=pltpu.VMEM),
            scratch_shapes=[
                pltpu.VMEM((nvec, sectors, blk, blk), BF16),
                pltpu.VMEM((2, nvec, 3, blk, blk), BF16),
                pltpu.VMEM((sectors, count, blk, blk), BF16),
                pltpu.VMEM((sectors, count, blk, blk), BF16),
                pltpu.VMEM((blk, blk), BF16),
                pltpu.VMEM((nvec, blk, count * blk), BF16),
                pltpu.VMEM((blk, count * blk), BF16),
                pltpu.VMEM((2, nvec, 4, 2, part, blk), F32),
                pltpu.VMEM((sectors, nvec, 4, part, blk), BF16),
                pltpu.VMEM((sectors, nvec, 4, part, blk), BF16),
                pltpu.VMEM((sectors, 2, 4, nvec, part, half), BF16),
                pltpu.VMEM((sectors, 2, 4, nvec, part, half), F32),
                pltpu.VMEM((sectors, 4, nvec, part, half), BF16),
                pltpu.VMEM((sectors, 3, nvec, part, half), BF16),
                pltpu.VMEM((sectors, nvec, part, half), F32),
                pltpu.VMEM((3, sectors, nvec, part, half), BF16),
                pltpu.VMEM((2, 128, 128), F32),
                pltpu.VMEM((2, nvec * 2, nyx * 8, 128), F32),
                pltpu.VMEM((nyx, 16, nvec * blk), BF16),
                pltpu.VMEM((nyx, 16, nvec * blk), BF16),
                dma,
                dma((2, sectors)),
                dma((2,)),
                dma((2, nvec)), dma((2, nvec)), dma((2, nvec)), dma((2, nvec)),
                dma((sectors,)), dma((sectors,)), dma((sectors,)), dma((sectors,)),
                dma((sectors, 3)), dma((sectors, 3)),
                dma((nyx,)), dma((nyx,)),
                dma,
            ],
            compiler_params=pltpu.CompilerParams(
                collective_id=0, has_side_effects=True, vmem_limit_bytes=56 * 1024 * 1024
            ),
        )(shifts, active, psi, left_ops, right_ops)
        return result.reshape(nvec, blk // nsec, blk // 8, blk).transpose(0, 1, 3, 2)

    return jax.shard_map(
        per_device,
        mesh=mesh,
        in_specs=(
            P(None, "sec", None, None),
            P("op", "sec", None, None),
            P("op", "sec", None, None),
            P("op"),
            P("op", "sec"),
        ),
        out_specs=P(None, "sec", None, "op"),
        check_vma=False,
    )
```

time: 269 us -> 68.5 us (0.25)
  blocking collectives: 165 us -> 0 us
  Pallas kernels: 0 us -> 66.6 us
  matrix products: 33.7 us -> 0 us
  waiting for transfers between devices: 24 us -> 0 us
  local copies, waits for them, and re-layouts: 22.6 us -> 1.77 us
  starting transfers between devices: 11.7 us -> 0 us
  other arithmetic: 6 us -> 0 us
  loops' own time: 5.21 us -> 0 us
    psum x1 -> x0, blocking collectives: 132 us -> none  [per_device(): summed = lax.psum(total, 'op')]
    pallas_call x0 -> x1, Pallas kernels: none -> 66.6 us  [per_device(): pl.pallas_call(functools.partial(kernel, nsec * sectors, sizes), out_shap...]
    dot_general x4 -> x0, matrix products: 33.7 us -> none  [add_term(): jnp.einsum('vtik,tlk->vlti', middle, right_ops[index], preferred_element_...]
    all_to_all x1 -> x0, blocking collectives: 32.8 us -> none  [per_device(): lax.all_to_all(owned.astype(jnp.bfloat16), 'sec', split_axis=1, concat_ax...]
    ppermute x2 -> x0, waiting for transfers between devices: 24 us -> none  [the longest x1 16.8 us: extended(): after = lax.ppermute(leading, axis, down)]
    ppermute x2 -> x0, starting transfers between devices: 11.7 us -> none  [the longest x1 10.4 us: extended(): before = lax.ppermute(last, axis, up)]
    while x1 -> x0, local copies, waits for them, and re-layouts: 9.08 us -> none  [per_device(): lax.fori_loop(0, count, add_term, jnp.zeros((nvec, blk, sectors, blk), jn...]
    unnamed x6 -> x1, local copies, waits for them, and re-layouts: 8.67 us -> 1.77 us
  transfers between devices with their start and end apart: 2 -> 0, of which waited for: 2 -> 0; matrix products, arithmetic and copies ran while one was open for 0% -> 0% of each run, Pallas kernels for 0% -> 0%
where the time goes in v1:
time: 68.5 us; the launch traced here: 68.4 us
  Pallas kernels  66.6 us (97%)
  local copies, waits for them, and re-layouts  1.77 us (3%)
    pallas_call x1, Pallas kernels, per_device(): pl.pallas_call(functools.partial(kernel, nsec * sectors, sizes), out_shap...  66.6 us
    unnamed x1, local copies, waits for them, and re-layouts  1.77 us

profile of v1, /device:TPU:1, one launch (start us, length us, event | category | flops | bytes accessed | tf_op | source)
XLA Modules:
  0.0 68.4 jit_solution(940547120859495598)
XLA Ops:
  0.0 66.6 %shard_map.55 = bf16[768,256]{1,0:T(8,128)(2,1)} custom-call(s32[4]{0:T(128)} %shifts.1, s32[4,8]{1,0:T(4,128)} %active.1, bf16[3,8,256,256]{3,2,1,0:T(8,128)(2,1)} %psi_hbm.1, bf16[4,8,256,256]{3,2,1,0:T(8,128)(2,1)} %left_hbm.1, bf16[4,8,256,256]{3,2,1,0:T(8,128)(2,1)} %right_hbm.1), custom_call_target="tpu_custom_call" | custom-call | tf_op jit(solution)/shard_map/pallas_call | solution.py:346
  66.6 1.8 %copy.7 = bf16[3,8,256,32]{2,3,1,0:T(8,128)(2,1)} copy(bf16[3,8,256,32]{2,3,1,0:T(8,128)(2,1)} %bitcast.3) | data formatting | bytes 786432

commit v2 on v1

--- a/solution.py
+++ b/solution.py
@@ -10,17 +10,20 @@
 MESH = pl.DeviceIdType.MESH
 F32 = jnp.float32
 BF16 = jnp.bfloat16
-LAG = 2
+LAG = 4
+RELAY = 2
+EARLY = False
 
 
 def kernel(
     nsec_total, sizes, shifts, active, psi_hbm, left_hbm, right_hbm, out_ref,
     psi, edge, left, right, perm, mid, rcat, acc,
-    s0, r0, s1, keep, r1, s2, own, r2, turn, wide, wsend, wrecv,
+    s0, r0, s1, keep, r1, s2, own, r2, turn, wide, wsend, wrecv, order, flat,
     load_sem, op_sem, edge_sem, halo_send, halo_recv, sib_send, sib_recv,
     send0, recv0, send1, recv1, send2, recv2, send3, recv3, self_sem,
 ):
     nyx, count, nvec, sectors, blk = sizes
+    assert (nyx, sectors, blk) == (16, 8, 256)
     op, sec = lax.axis_index("op"), lax.axis_index("sec")
     zl, core = lax.div(op, 2), lax.rem(op, 2)
     yx, zh = lax.div(sec, 2), lax.rem(sec, 2)
@@ -37,19 +40,26 @@
     sibling = {"op": zl * 2 + other, "sec": sec}
     partner = at(z + 1 - 2 * e, yx)
     sec_up, sec_down = lax.rem(sec + 1, nsec), lax.rem(sec + nsec - 1, nsec)
-    ahead = {
-        "op": jnp.where(zl == 3, core, op + 2),
-        "sec": jnp.where(zl == 3, sec_up, sec),
-    }
-    behind = {
-        "op": jnp.where(zl == 0, 6 + core, op - 2),
-        "sec": jnp.where(zl == 0, sec_down, sec),
-    }
+
+    def chain(zls, secs):
+        pick = lambda w: jnp.where(zl == 0, w[0], jnp.where(zl == 1, w[1], jnp.where(zl == 2, w[2], w[3])))
+        return {"op": pick(zls) * 2 + core, "sec": pick(secs)}
+
+    halo_to = (
+        chain((2, 2, 1, 1), (sec_down, sec, sec, sec_up)),
+        chain((3, 3, 0, 0), (sec_down, sec, sec, sec_up)),
+        chain((3, 3, 0, 0), (sec_up, sec, sec, sec_down)),
+    )
+    greets = (
+        chain((2, 3, 0, 1), (sec_down, sec_down, sec_up, sec_up)),
+        chain((3, 2, 1, 0), (sec_down, sec, sec, sec_up)),
+        chain((3, 2, 1, 0), (sec_up, sec, sec, sec_down)),
+    )
 
     barrier = pltpu.get_barrier_semaphore()
     pl.semaphore_signal(barrier, inc=1, device_id=sibling, device_id_type=MESH)
-    pl.semaphore_signal(barrier, inc=1, device_id=ahead, device_id_type=MESH)
-    pl.semaphore_signal(barrier, inc=1, device_id=behind, device_id_type=MESH)
+    for peer in greets:
+        pl.semaphore_signal(barrier, inc=1, device_id=peer, device_id_type=MESH)
 
     @pl.loop(1, 8)
     def _(d):
@@ -87,66 +97,51 @@
     for copy in edge_loads:
         copy.start()
 
-    rows_each = blk // nsec
     row = lax.broadcasted_iota(jnp.int32, (blk, blk), 0)
     col = lax.broadcasted_iota(jnp.int32, (blk, blk), 1)
-    inner = lax.rem(row, half)
-    want = (
-        lax.div(inner, rows_each) * (2 * rows_each)
-        + lax.div(row, half) * rows_each
-        + lax.rem(inner, rows_each)
-    )
+    want = ((row & 120) << 1) | ((row & 128) >> 4) | (row & 7)
     perm[...] = jnp.where(col == want, 1.0, 0.0).astype(BF16)
 
-    load_psi.wait()
-    pl.semaphore_wait(barrier, 3 + 7 + nyx - 1)
+    turn_n = ((row & 128) >> 5) | (row & 3)
+    sector = jnp.where(turn_n < 6, turn_n + 1, jnp.where(turn_n == 6, 0, 7))
+    group = jnp.where(zh == 1, 1 - ((row & 4) >> 2), (row & 4) >> 2)
+    order[...] = jnp.where(
+        col == ((row & 120) << 1) + group * 8 + sector, 1.0, 0.0
+    ).astype(BF16)
+
 
     mine = pl.ds(core * half, half)
-
-    def halo(side, v, source):
+    role = 1 - e
+
+    def halo(side, v, hop, source):
         return pltpu.make_async_remote_copy(
             src_ref=source,
             dst_ref=edge.at[side, v, 2 * side, mine],
-            send_sem=halo_send.at[side, v],
+            send_sem=halo_send.at[hop, v],
             recv_sem=halo_recv.at[side, v],
-            device_id=behind if side else ahead,
+            device_id=halo_to[hop],
             device_id_type=MESH,
         )
 
-    def share(side, v):
+    def halo_in(side, v):
         return pltpu.make_async_remote_copy(
             src_ref=edge.at[side, v, 2 * side, mine],
             dst_ref=edge.at[side, v, 2 * side, mine],
-            send_sem=sib_send.at[side, v],
-            recv_sem=sib_recv.at[side, v],
+            send_sem=halo_send.at[0, v],
+            recv_sem=halo_recv.at[side, v],
             device_id=sibling,
             device_id_type=MESH,
         )
 
-    @pl.when(zl == 3)
-    def _():
-        for v in range(nvec):
-            halo(0, v, psi.at[v, sectors - 1, mine]).start()
-
-    @pl.when(zl == 0)
-    def _():
-        for v in range(nvec):
-            halo(1, v, psi.at[v, 0, mine]).start()
-
-    def relay(side, n):
-        place = (3 - zl) if side else zl
-        v = n - place
-
-        @pl.when((v >= 0) & (v < nvec))
-        def _():
-            here = edge.at[side, v, 2 * side, mine]
-            halo(side, v, here).wait_recv()
-
-            @pl.when(place < 3)
-            def _():
-                halo(side, v, here).start()
-
-            share(side, v).start()
+    def share(side):
+        return pltpu.make_async_remote_copy(
+            src_ref=edge.at[side, :, 2 * side, mine],
+            dst_ref=edge.at[side, :, 2 * side, mine],
+            send_sem=sib_send.at[side],
+            recv_sem=sib_recv.at[side],
+            device_id=sibling,
+            device_id_type=MESH,
+        )
 
     def compute(t, slot, source):
         for k in range(count):
@@ -212,123 +207,178 @@
                 s2[t, p - 1] = value.astype(BF16)
                 level2(t, p).start()
 
-    @pl.loop(0, sectors + LAG)
-    def _(n):
-        slot = lax.rem(n, 2)
-
-        @pl.when(n < sectors)
-        def _():
+    inner = sectors - 2
+    gap = LAG - 2
+    def first():
+        load_psi.wait()
+        for copy in load_ops(1):
+            copy.wait()
+        compute(1, 0, lambda v, shift: psi[v, 1 - shift])
+
+    if EARLY:
+        first()
+    pl.semaphore_wait(barrier, 4 + 7 + nyx - 1)
+    for zl_from, side in ((3, 0), (0, 1)):
+        @pl.when(zl == zl_from)
+        def _():
+            for hop, to_side in ((0, side), (1, side), (2, 1 - side)):
+                for v in range(nvec):
+                    source = psi_hbm.at[v, 0 if to_side else sectors - 1, mine]
+                    halo(to_side, v, hop, source).start()
+
+    if not EARLY:
+        first()
+    stage0(0, 0)
+
+    @pl.loop(1, sectors + LAG)
+    def _(m):
+        @pl.when(m < inner)
+        def _():
+            t = sector_of(m)
+            for copy in load_ops(t):
+                copy.wait()
+            compute(t, lax.rem(m, 2), lambda v, shift: psi[v, t - shift])
+            stage0(m, lax.rem(m, 2))
+
+        @pl.when(m == inner + gap)
+        def _():
+            for copy in edge_loads:
+                copy.wait()
+            for side in range(2):
+                share(side).wait_recv()
+
+        @pl.when((m >= inner + gap) & (m < sectors + gap))
+        def _():
+            n = m - gap
             t = sector_of(n)
             for copy in load_ops(t):
                 copy.wait()
-
-            @pl.when(n < sectors - 2)
+            which = n - inner
+            compute(t, lax.rem(n, 2), lambda v, shift: edge[which, v, 1 - shift])
+            stage0(n, lax.rem(n, 2))
+
+        @pl.when(m <= inner)
+        def _():
+            stage1(m - 1, lax.rem(m - 1, 2))
+
+        @pl.when((m > inner + gap) & (m <= sectors + gap))
+        def _():
+            n = m - 1 - gap
+            stage1(n, lax.rem(n, 2))
+
+        @pl.when((m >= RELAY) & (m < RELAY + nvec) & ((zl == 1) | (zl == 2)))
+        def _():
+            v = m - RELAY
+            halo_in(role, v).wait_recv()
+            halo(role, v, 0, edge.at[role, v, 2 * role, mine]).start()
+
+            @pl.when(v == nvec - 1)
             def _():
-                compute(t, slot, lambda v, shift: psi[v, t - shift])
-
-            @pl.when(n == sectors - 2)
-            def _():
-                for copy in edge_loads:
-                    copy.wait()
-                for side in range(2):
+                share(role).start()
+
+        @pl.when(m >= LAG)
+        def _():
+            stage2(m - LAG)
+
+        @pl.when(m == inner + gap - 1)
+        def _():
+            for side in range(2):
+                @pl.when((zl == 0) | (zl == 3) | (role != side))
+                def _():
                     for v in range(nvec):
-                        share(side, v).wait_recv()
-
-            @pl.when(n >= sectors - 2)
-            def _():
-                which = n - (sectors - 2)
-                compute(t, slot, lambda v, shift: edge[which, v, 1 - shift])
-
-            stage0(t, slot)
-
-        @pl.when(n < sectors - 2)
-        def _():
-            relay(0, n)
-            relay(1, n)
-
-        @pl.when((n >= 1) & (n <= sectors))
-        def _():
-            stage1(sector_of(n - 1), 1 - slot)
-
-        @pl.when(n >= LAG)
-        def _():
-            stage2(sector_of(n - LAG))
+                        halo_in(side, v).wait_recv()
+                    share(side).start()
 
     near = jnp.where(lax.rem(e + lax.div(zl, 2), 2) == 1, 0, 1)
-    for p in range(1, 4):
-        @pl.loop(0, sectors)
-        def _(t):
-            level2(t, p).wait_recv()
-
     part = blk // 8
-    for mine_group in (True, False):
-        group = zh if mine_group else 1 - zh
+
+    def spread(batch, d):
+        far = lax.rem(yx + d, nyx)
+        return pltpu.make_async_remote_copy(
+            src_ref=wsend.at[batch, far], dst_ref=wrecv.at[batch, yx],
+            send_sem=send3.at[batch, d], recv_sem=recv3.at[batch, d],
+            device_id=at(z, far), device_id_type=MESH,
+        )
+
+    def keep_own(batch):
+        return pltpu.make_async_copy(
+            wsend.at[batch, yx], wrecv.at[batch, yx], self_sem.at[batch]
+        )
+
+    for batch in range(2):
+        ns = slice(batch * 4, batch * 4 + 4)
+
+        @pl.loop(batch * 4, batch * 4 + 4)
+        def _(n):
+            for p in range(1, 4):
+                level2(n, p).wait_recv()
 
         @pl.loop(0, nvec)
         def _(v):
-            for quad in range(2):
-                ts = slice(quad * 4, quad * 4 + 4)
-                if mine_group:
-                    value = own[ts, v] + r2[near, ts, v].astype(F32)
+            for group in range(2):
+                if group == 0:
+                    value = own[ns, v] + r2[near, ns, v].astype(F32)
                 else:
-                    value = r2[1 - near, ts, v].astype(F32) + r2[2, ts, v].astype(F32)
-                turn[quad] = value.reshape(4 * part, half).T
+                    value = r2[1 - near, ns, v].astype(F32) + r2[2, ns, v].astype(F32)
+                turn[group] = value.reshape(4 * part, half).T
                 for lq in range(2):
-                    pieces = [turn[quad, pl.ds(lq * 4 + r, nyx, stride=8), :] for r in range(4)]
-                    for t4 in range(4):
-                        lanes = slice(t4 * part, (t4 + 1) * part)
+                    pieces = [turn[group, pl.ds(lq * 4 + r, nyx, stride=8), :] for r in range(4)]
+                    for n4 in range(4):
+                        lanes = slice(n4 * part, (n4 + 1) * part)
                         joined = jnp.concatenate([piece[:, lanes] for piece in pieces], axis=1)
-                        wide[group, v * 2 + lq, pl.ds(quad * 4 + t4, nyx, stride=8), :] = joined
-
-    @pl.loop(0, nyx)
-    def _(d):
-        rows = pl.ds(pl.multiple_of(d * 8, 8), 8)
-        for tile in range(6):
-            both = [wide[group, tile, rows, :] for group in range(2)]
-            lanes = slice(tile * 128, (tile + 1) * 128)
-            wsend[d, :, lanes] = jnp.concatenate(both, axis=0).astype(BF16)
-
-    def spread(d):
-        far = lax.rem(yx + d, nyx)
-        return pltpu.make_async_remote_copy(
-            src_ref=wsend.at[far], dst_ref=wrecv.at[yx],
-            send_sem=send3.at[d], recv_sem=recv3.at[d],
-            device_id=at(z, far), device_id_type=MESH,
-        )
-
-    @pl.loop(1, nyx)
-    def _(d):
-        spread(d).start()
-
-    keep_own = pltpu.make_async_copy(wsend.at[yx], wrecv.at[yx], self_sem)
-    keep_own.start()
-    keep_own.wait()
-
-    @pl.loop(1, nyx)
-    def _(d):
-        spread(d).wait_recv()
-
-    for h in range(2):
+                        wide[batch, v * 2 + lq, pl.ds(group * 4 + n4, nyx, stride=8), :] = joined
+
         for tile in range(6):
             lanes = slice(tile * 128, (tile + 1) * 128)
-            value = wrecv[h * 8 : (h + 1) * 8, :, lanes].astype(F32).reshape(128, 128)
-            out_ref[lanes, h * 128 : (h + 1) * 128] = value.T.astype(BF16)
+            wsend[batch, :, :, lanes] = wide[batch, tile].reshape(nyx, 8, 128).astype(BF16)
+
+        @pl.loop(1, nyx)
+        def _(d):
+            spread(batch, d).start()
+
+        keep_own(batch).start()
+
+    for batch in range(2):
+        keep_own(batch).wait()
+
+        @pl.loop(1, nyx)
+        def _(d):
+            spread(batch, d).wait_recv()
+
+        for tile in range(6):
+            lanes = slice(tile * 128, (tile + 1) * 128)
+            value = wrecv[batch, :, :, lanes].astype(F32).reshape(128, 128)
+            flat[lanes, batch * 128 : (batch + 1) * 128] = value.T.astype(BF16)
+
+    for v in range(nvec):
+        rows = slice(v * blk, (v + 1) * blk)
+        out_ref[rows] = jnp.dot(
+            flat[rows], order[...], preferred_element_type=F32
+        ).astype(BF16)
+
+    for v in range(nvec):
+        halo(role, v, 0, edge.at[role, v, 2 * role, mine]).wait_send()
+
+    @pl.when((zl == 0) | (zl == 3))
+    def _():
+        for hop in (1, 2):
+            for v in range(nvec):
+                halo(role, v, hop, edge.at[role, v, 2 * role, mine]).wait_send()
 
     for side in range(2):
-        for v in range(nvec):
-            halo(side, v, psi.at[v, 0, mine]).wait_send()
-            share(side, v).wait_send()
+        share(side).wait_send()
 
     @pl.loop(0, sectors)
-    def _(t):
-        level0(t).wait_send()
-        level1(t).wait_send()
+    def _(n):
+        level0(n).wait_send()
+        level1(n).wait_send()
         for p in range(1, 4):
-            level2(t, p).wait_send()
-
-    @pl.loop(1, nyx)
-    def _(d):
-        spread(d).wait_send()
+            level2(n, p).wait_send()
+
+    for batch in range(2):
+        @pl.loop(1, nyx)
+        def _(d):
+            spread(batch, d).wait_send()
 
 
 def solution(mesh):
@@ -367,16 +417,18 @@
                 pltpu.VMEM((3, sectors, nvec, part, half), BF16),
                 pltpu.VMEM((2, 128, 128), F32),
                 pltpu.VMEM((2, nvec * 2, nyx * 8, 128), F32),
-                pltpu.VMEM((nyx, 16, nvec * blk), BF16),
-                pltpu.VMEM((nyx, 16, nvec * blk), BF16),
+                pltpu.VMEM((2, nyx, 8, nvec * blk), BF16),
+                pltpu.VMEM((2, nyx, 8, nvec * blk), BF16),
+                pltpu.VMEM((blk, blk), BF16),
+                pltpu.VMEM((nvec * blk, blk), BF16),
                 dma,
                 dma((2, sectors)),
                 dma((2,)),
-                dma((2, nvec)), dma((2, nvec)), dma((2, nvec)), dma((2, nvec)),
+                dma((3, nvec)), dma((2, nvec)), dma((2,)), dma((2,)),
                 dma((sectors,)), dma((sectors,)), dma((sectors,)), dma((sectors,)),
                 dma((sectors, 3)), dma((sectors, 3)),
-                dma((nyx,)), dma((nyx,)),
-                dma,
+                dma((2, nyx)), dma((2, nyx)),
+                dma((2,)),
             ],
             compiler_params=pltpu.CompilerParams(
                 collective_id=0, has_side_effects=True, vmem_limit_bytes=56 * 1024 * 1024

time: 68.5 us -> 58.9 us (0.86)
  Pallas kernels: 66.6 us -> 57 us
    pallas_call x1, Pallas kernels: 66.6 us -> 57 us  [per_device(): pl.pallas_call(functools.partial(kernel, nsec * sectors, sizes), out_shap...]
where the time goes in v2:
time: 58.9 us; the launch traced here: 58.7 us
  Pallas kernels  57 us (97%)
  local copies, waits for them, and re-layouts  1.77 us (3%)
    pallas_call x1, Pallas kernels, per_device(): pl.pallas_call(functools.partial(kernel, nsec * sectors, sizes), out_shap...  57 us
    unnamed x1, local copies, waits for them, and re-layouts  1.77 us

profile of v2, /device:TPU:1, one launch (start us, length us, event | category | flops | bytes accessed | tf_op | source)
XLA Modules:
  0.0 58.7 jit_solution(16278127759805917582)
XLA Ops:
  0.0 57.0 %shard_map.55 = bf16[768,256]{1,0:T(8,128)(2,1)} custom-call(s32[4]{0:T(128)} %shifts.1, s32[4,8]{1,0:T(4,128)} %active.1, bf16[3,8,256,256]{3,2,1,0:T(8,128)(2,1)} %psi_hbm.1, bf16[4,8,256,256]{3,2,1,0:T(8,128)(2,1)} %left_hbm.1, bf16[4,8,256,256]{3,2,1,0:T(8,128)(2,1)} %right_hbm.1), custom_call_target="tpu_custom_call" | custom-call | tf_op jit(solution)/shard_map/pallas_call | solution.py:396
  57.0 1.8 %copy.7 = bf16[3,8,256,32]{2,3,1,0:T(8,128)(2,1)} copy(bf16[3,8,256,32]{2,3,1,0:T(8,128)(2,1)} %bitcast.3) | data formatting | bytes 786432

commit v3 on v2

--- a/solution.py
+++ b/solution.py
@@ -16,9 +16,9 @@
 
 
 def kernel(
-    nsec_total, sizes, shifts, active, psi_hbm, left_hbm, right_hbm, out_ref,
+    nsec_total, sizes, shifts, active, psi_hbm, left_hbm, right_hbm, wrecv,
     psi, edge, left, right, perm, mid, rcat, acc,
-    s0, r0, s1, keep, r1, s2, own, r2, turn, wide, wsend, wrecv, order, flat,
+    s0, r0, s1, keep, r1, s2, own, r2, turn, wide, wsend,
     load_sem, op_sem, edge_sem, halo_send, halo_recv, sib_send, sib_recv,
     send0, recv0, send1, recv1, send2, recv2, send3, recv3, self_sem,
 ):
@@ -72,7 +72,6 @@
         )
 
     load_psi = pltpu.make_async_copy(psi_hbm, psi, load_sem)
-    load_psi.start()
 
     def sector_of(n):
         return jnp.where(n < sectors - 2, n + 1, jnp.where(n == sectors - 2, 0, sectors - 1))
@@ -83,7 +82,11 @@
             pltpu.make_async_copy(right_hbm.at[:, t], right.at[t], op_sem.at[1, t]),
         )
 
-    @pl.loop(0, sectors)
+    for copy in load_ops(1):
+        copy.start()
+    load_psi.start()
+
+    @pl.loop(1, sectors)
     def _(n):
         for copy in load_ops(sector_of(n)):
             copy.start()
@@ -101,14 +104,6 @@
     col = lax.broadcasted_iota(jnp.int32, (blk, blk), 1)
     want = ((row & 120) << 1) | ((row & 128) >> 4) | (row & 7)
     perm[...] = jnp.where(col == want, 1.0, 0.0).astype(BF16)
-
-    turn_n = ((row & 128) >> 5) | (row & 3)
-    sector = jnp.where(turn_n < 6, turn_n + 1, jnp.where(turn_n == 6, 0, 7))
-    group = jnp.where(zh == 1, 1 - ((row & 4) >> 2), (row & 4) >> 2)
-    order[...] = jnp.where(
-        col == ((row & 120) << 1) + group * 8 + sector, 1.0, 0.0
-    ).astype(BF16)
-
 
     mine = pl.ds(core * half, half)
     role = 1 - e
@@ -199,7 +194,7 @@
 
     def stage2(t):
         level1(t).wait_recv()
-        for p in range(4):
+        for p in (3, 2, 1, 0):
             value = keep[t, 1 - e, p] + r1[t, p].astype(F32)
             if p == 0:
                 own[t] = value
@@ -238,6 +233,7 @@
             for copy in load_ops(t):
                 copy.wait()
             compute(t, lax.rem(m, 2), lambda v, shift: psi[v, t - shift])
+            stage1(m - 1, lax.rem(m - 1, 2))
             stage0(m, lax.rem(m, 2))
 
         @pl.when(m == inner + gap)
@@ -257,7 +253,7 @@
             compute(t, lax.rem(n, 2), lambda v, shift: edge[which, v, 1 - shift])
             stage0(n, lax.rem(n, 2))
 
-        @pl.when(m <= inner)
+        @pl.when(m == inner)
         def _():
             stage1(m - 1, lax.rem(m - 1, 2))
 
@@ -293,7 +289,8 @@
     part = blk // 8
 
     def spread(batch, d):
-        far = lax.rem(yx + d, nyx)
+        y, x = lax.div(yx, 4), lax.rem(yx, 4)
+        far = lax.rem(y + lax.div(d, 4), 4) * 4 + lax.rem(x + lax.rem(d, 4), 4)
         return pltpu.make_async_remote_copy(
             src_ref=wsend.at[batch, far], dst_ref=wrecv.at[batch, yx],
             send_sem=send3.at[batch, d], recv_sem=recv3.at[batch, d],
@@ -332,9 +329,8 @@
             lanes = slice(tile * 128, (tile + 1) * 128)
             wsend[batch, :, :, lanes] = wide[batch, tile].reshape(nyx, 8, 128).astype(BF16)
 
-        @pl.loop(1, nyx)
-        def _(d):
-            spread(batch, d).start()
+        for d in sorted(range(1, nyx), key=lambda d: -(min(d // 4, 4 - d // 4) + min(d % 4, 4 - d % 4))):
+            spread(batch, jnp.int32(d)).start()
 
         keep_own(batch).start()
 
@@ -344,17 +340,6 @@
         @pl.loop(1, nyx)
         def _(d):
             spread(batch, d).wait_recv()
-
-        for tile in range(6):
-            lanes = slice(tile * 128, (tile + 1) * 128)
-            value = wrecv[batch, :, :, lanes].astype(F32).reshape(128, 128)
-            flat[lanes, batch * 128 : (batch + 1) * 128] = value.T.astype(BF16)
-
-    for v in range(nvec):
-        rows = slice(v * blk, (v + 1) * blk)
-        out_ref[rows] = jnp.dot(
-            flat[rows], order[...], preferred_element_type=F32
-        ).astype(BF16)
 
     for v in range(nvec):
         halo(role, v, 0, edge.at[role, v, 2 * role, mine]).wait_send()
@@ -379,6 +364,28 @@
         @pl.loop(1, nyx)
         def _(d):
             spread(batch, d).wait_send()
+
+
+def transpose_kernel(rows_ref, out_ref, flat):
+    zh = lax.rem(lax.axis_index("sec"), 2)
+    blk = out_ref.shape[1]
+    row = lax.broadcasted_iota(jnp.int32, (blk, blk), 0)
+    col = lax.broadcasted_iota(jnp.int32, (blk, blk), 1)
+
+    turn_n = ((row & 128) >> 5) | (row & 3)
+    sector = jnp.where(turn_n < 6, turn_n + 1, jnp.where(turn_n == 6, 0, 7))
+    group = jnp.where(zh == 1, 1 - ((row & 4) >> 2), (row & 4) >> 2)
+    order = jnp.where(
+        col == ((row & 120) << 1) + group * 8 + sector, 1.0, 0.0
+    ).astype(BF16)
+    for tile in range(out_ref.shape[0] // 128):
+        lanes = slice(tile * 128, (tile + 1) * 128)
+        for batch in range(2):
+            value = rows_ref[batch, :, :, lanes].astype(F32).reshape(128, 128)
+            flat[lanes, batch * 128 : (batch + 1) * 128] = value.T.astype(BF16)
+    for start in range(0, out_ref.shape[0], blk):
+        rows = slice(start, start + blk)
+        out_ref[rows] = jnp.dot(flat[rows], order, preferred_element_type=F32).astype(BF16)
 
 
 def solution(mesh):
@@ -395,9 +402,9 @@
         dma = pltpu.SemaphoreType.DMA
         result = pl.pallas_call(
             functools.partial(kernel, nsec * sectors, sizes),
-            out_shape=jax.ShapeDtypeStruct((nvec * blk, blk), BF16),
+            out_shape=jax.ShapeDtypeStruct((2, nyx, 8, nvec * blk), BF16),
             in_specs=[smem, smem, hbm, hbm, hbm],
-            out_specs=pl.BlockSpec(memory_space=pltpu.VMEM),
+            out_specs=hbm,
             scratch_shapes=[
                 pltpu.VMEM((nvec, sectors, blk, blk), BF16),
                 pltpu.VMEM((2, nvec, 3, blk, blk), BF16),
@@ -418,9 +425,6 @@
                 pltpu.VMEM((2, 128, 128), F32),
                 pltpu.VMEM((2, nvec * 2, nyx * 8, 128), F32),
                 pltpu.VMEM((2, nyx, 8, nvec * blk), BF16),
-                pltpu.VMEM((2, nyx, 8, nvec * blk), BF16),
-                pltpu.VMEM((blk, blk), BF16),
-                pltpu.VMEM((nvec * blk, blk), BF16),
                 dma,
                 dma((2, sectors)),
                 dma((2,)),
@@ -434,6 +438,13 @@
                 collective_id=0, has_side_effects=True, vmem_limit_bytes=56 * 1024 * 1024
             ),
         )(shifts, active, psi, left_ops, right_ops)
+        result = pl.pallas_call(
+            transpose_kernel,
+            out_shape=jax.ShapeDtypeStruct((nvec * blk, blk), BF16),
+            in_specs=[pl.BlockSpec(memory_space=pltpu.VMEM)],
+            out_specs=pl.BlockSpec(memory_space=pltpu.VMEM),
+            scratch_shapes=[pltpu.VMEM((nvec * blk, blk), BF16)],
+        )(result)
         return result.reshape(nvec, blk // nsec, blk // 8, blk).transpose(0, 1, 3, 2)
 
     return jax.shard_map(

time: 58.9 us -> 57 us (0.968)
  local copies, waits for them, and re-layouts: 1.77 us -> 0 us
    pallas_call x1, Pallas kernels: 57 us -> 54.7 us  [per_device(): pl.pallas_call(functools.partial(kernel, nsec * sectors, sizes), out_shap...]
    pallas_call x0 -> x1, Pallas kernels: none -> 2.14 us  [per_device(): pl.pallas_call(transpose_kernel, out_shape=jax.ShapeDtypeStruct((nvec * b...]
    unnamed x1 -> x0, local copies, waits for them, and re-layouts: 1.77 us -> none
where the time goes in v3:
time: 57 us; the launch traced here: 56.8 us
  Pallas kernels  56.8 us (100%)
    pallas_call x1, Pallas kernels, per_device(): pl.pallas_call(functools.partial(kernel, nsec * sectors, sizes), out_shap...  54.7 us
    pallas_call x1, Pallas kernels, per_device(): pl.pallas_call(transpose_kernel, out_shape=jax.ShapeDtypeStruct((nvec * b...  2.14 us

profile of v3, /device:TPU:1, one launch (start us, length us, event | category | flops | bytes accessed | tf_op | source)
XLA Modules:
  0.0 56.8 jit_solution(1211351149299102011)
XLA Ops:
  0.0 54.7 %shard_map.55.rows_ref = bf16[2,16,8,768]{3,2,1,0:T(8,128)(2,1)} custom-call(s32[4]{0:T(128)} %shifts.1, s32[4,8]{1,0:T(4,128)} %active.1, bf16[3,8,256,256]{3,2,1,0:T(8,128)(2,1)} %psi_hbm.1, bf16[4,8,256,256]{3,2,1,0:T(8,128)(2,1)} %left_hbm.1, bf16[4,8,256,256]{3,2,1,0:T(8,128)(2,1)} %right_hbm.1), custom_call_target="tpu_custom_call" | custom-call | tf_op jit(solution)/shard_map/pallas_call | solution.py:403
  54.7 2.1 %shard_map.56 = bf16[768,256]{1,0:T(8,128)(2,1)} custom-call(bf16[2,16,8,768]{3,2,1,0:T(8,128)(2,1)} %shard_map.55.rows_ref), custom_call_target="tpu_custom_call" | custom-call | tf_op jit(solution)/shard_map/pallas_call | solution.py:441

commit v4 on v3

--- a/solution.py
+++ b/solution.py
@@ -10,7 +10,7 @@
 MESH = pl.DeviceIdType.MESH
 F32 = jnp.float32
 BF16 = jnp.bfloat16
-LAG = 4
+LAG = 3
 RELAY = 2
 EARLY = False
 

time: 57 us -> 56.8 us (level)
  no operation moved by 1% of the time
where the time goes in v4:
time: 56.8 us; the launch traced here: 56.7 us
  Pallas kernels  56.7 us (100%)
    pallas_call x1, Pallas kernels, per_device(): pl.pallas_call(functools.partial(kernel, nsec * sectors, sizes), out_shap...  54.5 us
    pallas_call x1, Pallas kernels, per_device(): pl.pallas_call(transpose_kernel, out_shape=jax.ShapeDtypeStruct((nvec * b...  2.14 us

profile of v4, /device:TPU:1, one launch (start us, length us, event | category | flops | bytes accessed | tf_op | source)
XLA Modules:
  0.0 56.7 jit_solution(11841372762093275103)
XLA Ops:
  0.0 54.5 %shard_map.55.rows_ref = bf16[2,16,8,768]{3,2,1,0:T(8,128)(2,1)} custom-call(s32[4]{0:T(128)} %shifts.1, s32[4,8]{1,0:T(4,128)} %active.1, bf16[3,8,256,256]{3,2,1,0:T(8,128)(2,1)} %psi_hbm.1, bf16[4,8,256,256]{3,2,1,0:T(8,128)(2,1)} %left_hbm.1, bf16[4,8,256,256]{3,2,1,0:T(8,128)(2,1)} %right_hbm.1), custom_call_target="tpu_custom_call" | custom-call | tf_op jit(solution)/shard_map/pallas_call | solution.py:403
  54.5 2.1 %shard_map.56 = bf16[768,256]{1,0:T(8,128)(2,1)} custom-call(bf16[2,16,8,768]{3,2,1,0:T(8,128)(2,1)} %shard_map.55.rows_ref), custom_call_target="tpu_custom_call" | custom-call | tf_op jit(solution)/shard_map/pallas_call | solution.py:441

commit v5 on v4

--- a/solution.py
+++ b/solution.py
@@ -161,9 +161,11 @@
             device_id=sibling, device_id_type=MESH,
         )
 
-    def level1(t):
-        return pltpu.make_async_remote_copy(
-            src_ref=s1.at[t, e], dst_ref=r1.at[t], send_sem=send1.at[t], recv_sem=recv1.at[t],
+    def level1(t, far):
+        places = pl.ds(2 * far, 2)
+        return pltpu.make_async_remote_copy(
+            src_ref=s1.at[t, e, places], dst_ref=r1.at[t, places],
+            send_sem=send1.at[t, far], recv_sem=recv1.at[t, far],
             device_id=partner, device_id_type=MESH,
         )
 
@@ -190,11 +192,13 @@
                 place = jnp.where(low, delta - 1, lax.rem(8 - delta, 8))
                 s1[t, side, place] = value.astype(BF16)
                 keep[t, side, place] = value
-        level1(t).start()
+        for far in (1, 0):
+            level1(t, far).start()
 
     def stage2(t):
-        level1(t).wait_recv()
         for p in (3, 2, 1, 0):
+            if p % 2:
+                level1(t, p // 2).wait_recv()
             value = keep[t, 1 - e, p] + r1[t, p].astype(F32)
             if p == 0:
                 own[t] = value
@@ -356,7 +360,8 @@
     @pl.loop(0, sectors)
     def _(n):
         level0(n).wait_send()
-        level1(n).wait_send()
+        for far in range(2):
+            level1(n, far).wait_send()
         for p in range(1, 4):
             level2(n, p).wait_send()
 
@@ -429,7 +434,7 @@
                 dma((2, sectors)),
                 dma((2,)),
                 dma((3, nvec)), dma((2, nvec)), dma((2,)), dma((2,)),
-                dma((sectors,)), dma((sectors,)), dma((sectors,)), dma((sectors,)),
+                dma((sectors,)), dma((sectors,)), dma((sectors, 2)), dma((sectors, 2)),
                 dma((sectors, 3)), dma((sectors, 3)),
                 dma((2, nyx)), dma((2, nyx)),
                 dma((2,)),

time: 56.8 us -> 57 us (level)
  no operation moved by 1% of the time
where the time goes in v5:
time: 57 us; the launch traced here: 56.9 us
  Pallas kernels  56.9 us (100%)
    pallas_call x1, Pallas kernels, per_device(): pl.pallas_call(functools.partial(kernel, nsec * sectors, sizes), out_shap...  54.7 us
    pallas_call x1, Pallas kernels, per_device(): pl.pallas_call(transpose_kernel, out_shape=jax.ShapeDtypeStruct((nvec * b...  2.14 us

profile of v5, /device:TPU:1, one launch (start us, length us, event | category | flops | bytes accessed | tf_op | source)
XLA Modules:
  0.0 56.9 jit_solution(13594886492579171915)
XLA Ops:
  0.0 54.7 %shard_map.55.rows_ref = bf16[2,16,8,768]{3,2,1,0:T(8,128)(2,1)} custom-call(s32[4]{0:T(128)} %shifts.1, s32[4,8]{1,0:T(4,128)} %active.1, bf16[3,8,256,256]{3,2,1,0:T(8,128)(2,1)} %psi_hbm.1, bf16[4,8,256,256]{3,2,1,0:T(8,128)(2,1)} %left_hbm.1, bf16[4,8,256,256]{3,2,1,0:T(8,128)(2,1)} %right_hbm.1), custom_call_target="tpu_custom_call" | custom-call | tf_op jit(solution)/shard_map/pallas_call | solution.py:408
  54.8 2.1 %shard_map.56 = bf16[768,256]{1,0:T(8,128)(2,1)} custom-call(bf16[2,16,8,768]{3,2,1,0:T(8,128)(2,1)} %shard_map.55.rows_ref), custom_call_target="tpu_custom_call" | custom-call | tf_op jit(solution)/shard_map/pallas_call | solution.py:446
